TPU v7x, 256 devices: a whole 4x4x8 slice. The times are simulated.
256 devices in a mesh: dp: 16 (over x, y), expert: 16 (over z, core).
Axes of the slice: x: 4, y: 4, z: 8, core: 2. Of those that a mesh axis runs over, the one named last changes fastest.
Arguments:
- item_feats: bfloat16 [16, 8192, 256], P('expert', 'dp'), may hold values from -6 to 6
- expert_ids: int32 [16, 8192, 1], P('expert', 'dp'), may hold values from 0 to 63; in each aligned block of 512 rows (0 to 511, 512 to 1023, ..., all dimensions but the last counted through in order) at most 32 rows name the same one
- weight_in: bfloat16 [64, 256, 1024], P('expert'), may hold values from -0.375 to 0.375
- weight_out: bfloat16 [64, 1024, 256], P('expert'), may hold values from -0.1875 to 0.1875
- queries: bfloat16 [16, 8192, 256], P('expert', 'dp'), may hold values from -150 to 150
- query_weight: float32 [16, 8192], P('expert', 'dp'), may hold values from 0.25 to 2
- positives: int32 [16, 8192], P('expert', 'dp'), may hold values from 0 to 8191
- sample_counts: int32 [16, 8192], P('expert'), may hold values from 1 to 4095
Outputs:
- query_loss: float32 [16, 8192], P('expert', 'dp')
- grad_queries: float32 [16, 8192, 256], P('expert', 'dp')
- grad_items: float32 [16, 8192, 256], P('expert', 'dp')
- grad_weight_in: float32 [256, 64, 1024], P('dp', 'expert')
- grad_weight_out: float32 [1024, 64, 256], P('dp', 'expert')
Inputs may be any that keep to these rules, and one draw needn't show every extreme that they name: `expert_ids`: the 512 items of one device name each expert at most 32 times.
All inputs are finite; a program needn't handle non-finite values.
Results may differ from a plain program's by a relative error of at most 0.023.
The roundings to bfloat16 on the way count: a program that leaves them out, or rounds other values in their place, can miss the bound.
Values may be sent and summed in bfloat16 or wider, within the bound.
A program may use at most 128 MiB of HBM per device.

v0:
```python
import jax
import jax.numpy as jnp
from jax import lax
from jax.sharding import Mesh
from jax.sharding import PartitionSpec as P

CAP = 32
DP = ("dp_0", "dp_1")


norm_eps = 1e-06


def whole_of(shard, axes, dim):
    whole = shard
    for number in range(len(axes) - 1, -1, -1):
        whole = lax.all_gather(whole, axes[number], axis=dim, tiled=True)
    return whole


def turned_gather(arrays, axis, dims):
    turned = [jnp.moveaxis(a, dim, 0) for a, dim in zip(arrays, dims)]
    widths = [t[0].size for t in turned]
    both = jnp.concatenate([t.reshape(-1, w) for t, w in zip(turned, widths)], axis=1)
    whole = lax.all_gather(both, axis, axis=0, tiled=True)
    pieces = jnp.split(whole, [sum(widths[:k]) for k in range(1, len(widths))], axis=1)
    return tuple(
        (
            jnp.moveaxis(b.reshape(-1, *t.shape[1:]), 0, dim)
            for b, t, dim in zip(pieces, turned, dims)
        )
    )


def in_blocks(shard, dim, peers):
    before, after = (shard.shape[:dim], shard.shape[dim + 1 :])
    return jnp.moveaxis(shard.reshape(*before, peers, -1, *after), dim, 0)


def sum_at_owner(shard, axis, dim):
    peers = lax.axis_size(axis)
    pieces = lax.all_to_all(in_blocks(shard, dim, peers), axis, 0, 0, tiled=True)
    return jnp.sum(pieces.astype(jnp.float32), axis=0)


def per_device(
    item_feats, expert_ids, weight_in, weight_out, queries, query_weight, positives, sample_counts
):
    groups = lax.axis_size("expert")
    shards = lax.axis_size(DP)
    local_experts = weight_in.shape[0]
    experts_all = local_experts * groups
    item_rows = item_feats.shape[1]
    feat_width = item_feats.shape[2]
    query_rows = queries.shape[1]
    slots_per = CAP
    features = item_feats[0].astype(jnp.float32)
    routes = expert_ids[0, :, 0]
    inv_rms = lax.rsqrt(jnp.mean(features * features, axis=1, keepdims=True) + norm_eps)
    normed = (features * inv_rms).astype(jnp.bfloat16)
    onehot = (routes[:, None] == jnp.arange(experts_all, dtype=jnp.int32)[None, :]).astype(
        jnp.int32
    )
    before = jnp.cumsum(onehot, axis=0) - onehot
    places = routes * slots_per + jnp.sum(before * onehot, axis=1)

    def scatter_slots(values):
        empty = jnp.zeros((experts_all * slots_per, feat_width), jnp.bfloat16)
        return empty.at[places].set(values).reshape(groups, local_experts, slots_per, feat_width)

    expert_received = lax.all_to_all(
        scatter_slots(normed), "expert", split_axis=0, concat_axis=0, tiled=True
    )
    hidden = jnp.einsum(
        "skcd,kdf->skcf", expert_received, weight_in, preferred_element_type=jnp.float32
    )
    expert_active = jax.nn.gelu(hidden).astype(jnp.bfloat16)
    output = jnp.einsum(
        "skcf,kfd->skcd", expert_active, weight_out, preferred_element_type=jnp.float32
    ).astype(jnp.bfloat16)
    output, received, active, hidden = (output, expert_received, expert_active, hidden)
    returned = lax.all_to_all(output, "expert", split_axis=0, concat_axis=0, tiled=True)
    branch = returned.reshape(experts_all * slots_per, feat_width)[places].astype(jnp.float32)
    reduced_sum = features + branch
    length = jnp.sqrt(jnp.sum(reduced_sum * reduced_sum, axis=1, keepdims=True) + norm_eps)
    unit_vecs = reduced_sum / length
    unit_low = unit_vecs.astype(jnp.bfloat16)
    query_matrix = queries[0]
    weights = query_weight[0]
    targets = positives[0]
    log_counts = jnp.log(sample_counts[0].astype(jnp.float32))
    shard_rows = lax.all_gather(unit_low, DP, axis=0, tiled=True)
    running = jnp.full((query_rows,), -jnp.inf, jnp.float32)
    totals = jnp.zeros((query_rows,), jnp.float32)
    row_count = shard_rows.shape[0]
    scores = (
        jnp.einsum("qd,kd->qk", query_matrix, shard_rows, preferred_element_type=jnp.float32)
        - log_counts[None, :]
    )
    highest = jnp.max(scores, axis=1)
    totals = totals * jnp.exp(running - highest) + jnp.sum(
        jnp.exp(scores - highest[:, None]), axis=1
    )
    columns = jnp.arange(row_count, dtype=jnp.int32)
    picked = jnp.sum(jnp.where(columns[None, :] == targets[:, None], scores, 0.0), axis=1)
    gathered, highest, totals, picked = (shard_rows, highest, totals, picked)
    log_total = highest + jnp.log(totals)
    query_loss = (log_total - picked)[None, :]
    block_layout = gathered.reshape(shards, item_rows, feat_width)
    counts_view = log_counts.reshape(shards, item_rows)

    def weigh_block(inputs):
        item_tile_rows, block_logs, first_item = inputs
        scores = (
            jnp.einsum(
                "qd,kd->qk", query_matrix, item_tile_rows, preferred_element_type=jnp.float32
            )
            - block_logs[None, :]
        )
        columns = first_item + jnp.arange(item_rows, dtype=jnp.int32)
        target_hit = (columns[None, :] == targets[:, None]).astype(jnp.float32)
        return (weights[:, None] * (jnp.exp(scores - log_total[:, None]) - target_hit)).astype(
            jnp.bfloat16
        )

    mixing_factors = lax.map(
        weigh_block, (block_layout, counts_view, jnp.arange(shards, dtype=jnp.int32) * item_rows)
    )
    grad_queries = jnp.einsum(
        "ira,ias->rs", mixing_factors, block_layout, preferred_element_type=jnp.float32
    )
    all_queries = whole_of(query_matrix, DP, 0)
    all_lse, all_weights, all_targets = turned_gather(
        (log_total, weights, targets.astype(jnp.float32)), DP, (0, 0, 0)
    )
    first_item = lax.axis_index(DP) * item_rows
    own_logs = lax.dynamic_slice_in_dim(log_counts, first_item, item_rows)
    scores = (
        jnp.einsum("qd,kd->qk", all_queries, unit_low, preferred_element_type=jnp.float32)
        - own_logs[None, :]
    )
    columns = first_item + jnp.arange(item_rows, dtype=jnp.int32)
    target_hit = (columns[None, :] == all_targets.astype(jnp.int32)[:, None]).astype(jnp.float32)
    terms = (all_weights[:, None] * (jnp.exp(scores - all_lse[:, None]) - target_hit)).astype(
        jnp.bfloat16
    )
    grad_unit = jnp.einsum("qk,qd->kd", terms, all_queries, preferred_element_type=jnp.float32)
    along = jnp.sum(unit_vecs * grad_unit, axis=1, keepdims=True)
    grad_summed = (grad_unit - unit_vecs * along) / length
    grad_low = grad_summed.astype(jnp.bfloat16)
    grad_in = lax.all_to_all(
        scatter_slots(grad_low), "expert", split_axis=0, concat_axis=0, tiled=True
    )
    grad_active = jnp.einsum(
        "skcd,kfd->skcf", grad_in, weight_out, preferred_element_type=jnp.float32
    )
    grad_hidden = jax.vjp(jax.nn.gelu, hidden)[1](grad_active)[0].astype(jnp.bfloat16)
    grad_normed = jnp.einsum(
        "skcf,kdf->skcd", grad_hidden, weight_in, preferred_element_type=jnp.float32
    ).astype(jnp.bfloat16)
    grad_back = lax.all_to_all(grad_normed, "expert", split_axis=0, concat_axis=0, tiled=True)
    grad_rows = grad_back.reshape(experts_all * slots_per, feat_width)[places].astype(jnp.float32)
    projected = jnp.mean(grad_rows * features, axis=1, keepdims=True)
    grad_items = grad_summed + inv_rms * (grad_rows - features * inv_rms * inv_rms * projected)
    cut_rows = received
    grad_weight_in = sum_at_owner(
        jnp.einsum(
            "skcr,skcf->rkf", cut_rows, grad_hidden, preferred_element_type=jnp.float32
        ).astype(jnp.bfloat16),
        DP,
        0,
    )
    cut_rows = active
    grad_weight_out = sum_at_owner(
        jnp.einsum("skcr,skcd->rkd", cut_rows, grad_in, preferred_element_type=jnp.float32).astype(
            jnp.bfloat16
        ),
        DP,
        0,
    )
    return (query_loss, grad_queries[None], grad_items[None], grad_weight_in, grad_weight_out)


def solution(mesh):
    torus = Mesh(mesh.devices.reshape(4, 4, mesh.shape["expert"]), ("dp_0", "dp_1", "expert"))
    in_specs = (
        P("expert", DP, None),
        P("expert", DP, None),
        P("expert", None, None),
        P("expert", None, None),
        P("expert", DP, None),
        P("expert", DP),
        P("expert", DP),
        P("expert", None),
    )
    out_specs = (
        P("expert", DP),
        P("expert", DP, None),
        P("expert", DP, None),
        P(DP, "expert", None),
        P(DP, "expert", None),
    )
    return jax.shard_map(
        per_device, mesh=torus, in_specs=in_specs, out_specs=out_specs, check_vma=False
    )
```

profile of v0, /device:TPU:24, one launch (start us, length us, event | category | flops | bytes accessed | tf_op | source)
XLA Modules:
  0.0 437.8 jit_solution(691531987160299539)
XLA Ops:
  13.1 3.1 scatter_custom_fusion
  16.2 35.6 %all_to_all.30 = bf16[16,4,32,256]{3,2,1,0:T(8,128)(2,1)S(1)} all-to-all(bf16[16,4,32,256]{3,2,1,0:T(8,128)(2,1)S(1)} %bitcast.222), channel_id=1, replica_groups=mesh['dp_0'=4,'dp_1'=4,'expert'=16] {'expert'}, dimensions={0} | all-to-all | bytes 2097152 | tf_op jit(solution)/shard_map/all_to_all | solution.py:71
  51.8 5.0 %fusion.26 = (bf16[16,4,32,1024]{3,2,0,1:T(8,128)(2,1)S(1)}, f32[4,16,32,1024]{3,2,1,0:T(8,128)}) fusion(bf16[4,256,1024]{2,1,0:T(8,128)(2,1)S(1)} %copy-done, bf16[16,4,32,256]{3,2,1,0:T(8,128)(2,1)S(1)} %all_to_all.30), kind=kOutput, calls=%fused_computation.43 | convolution fusion | flops 1092616192 | bytes 15728640 | tf_op jit(solution)/shard_map/skcd,kdf->skcf/dot_general | solution.py:74
  59.9 4.2 all-to-all-start.1
  64.9 25.8 %all-to-all-done.1 = bf16[16,4,32,256]{3,2,1,0:T(8,128)(2,1)S(1)} async-done(((bf16[16,4,32,256]{3,2,1,0:T(8,128)(2,1)}), bf16[16,4,32,256]{3,2,1,0:T(8,128)(2,1)S(1)}, u32[]{:S(2)}, u32[]{:S(2)}) %all-to-all-start.1) | async-done | bytes 1048608 | tf_op jit(solution)/shard_map/all_to_all | solution.py:82
  90.7 2.6 gather_fusion
  97.4 62.8 %all-gather.6.cloned.1.call-done = bf16[8192,256]{0,1:T(8,128)(2,1)} async-done(((bf16[512,256]{0,1:T(8,128)(2,1)}), bf16[8192,256]{0,1:T(8,128)(2,1)}) %all-gather.6.cloned.1.call-update) | async-done | bytes 4194320 | tf_op jit(solution)/shard_map/all_gather | solution.py:92
  160.2 5.4 %subtract_reduce_fusion = (f32[512]{0:T(512)S(1)}, f32[8192,512]{1,0:T(8,128)S(1)}) fusion(f32[8192]{0:T(1024)S(1)} %bitcast.225, bf16[8192,256]{0,1:T(8,128)(2,1)} %all-gather.6.cloned.1.call-done, bf16[1,512,256]{2,1,0:T(8,128)(2,1)} %param.14), kind=kOutput, calls=%fused_computation.27 | convolution fusion | flops 2155871744 | bytes 21268480 | tf_op jit(solution)/shard_map/qd,kd->qk/dot_general | solution.py:97
  165.7 5.4 %fusion.14 = (f32[512]{0:T(512)S(1)}, f32[512]{0:T(512)}) fusion(f32[8192,512]{1,0:T(8,128)S(1)} %get-tuple-element.96, f32[512]{0:T(512)S(1)} %get-tuple-element.95, f32[8192]{0:T(1024)S(1)} %bitcast.226, s32[512]{0:T(512)S(1)} %bitcast.241), kind=kLoop, calls=%fused_computation.24 | loop fusion | flops 25164800 | bytes 16818176 | tf_op jit(solution)/shard_map/reduce_sum | solution.py:101
  171.1 21.8 %all_gather.13 = f32[8192,3]{0,1:T(4,128)S(1)} all-gather(f32[512,3]{0,1:T(4,128)S(1)} %pad_maximum_fusion), channel_id=1, replica_groups=mesh['dp_0'=4,'dp_1'=4,'expert'=16] {'dp_0','dp_1'}, dimensions={0}, use_global_device_ids=true | all-gather | bytes 104448 | tf_op jit(solution)/shard_map/all_gather | solution.py:25
  193.0 20.3 %all-gather.10.cloned.1.call-done = bf16[1,8192,256]{2,1,0:T(8,128)(2,1)} async-done(((bf16[1,2048,256]{2,1,0:T(8,128)(2,1)}), bf16[1,8192,256]{2,1,0:T(8,128)(2,1)}) %all-gather.10.cloned.1.call-update) | async-done | bytes 4194320 | tf_op jit(solution)/shard_map/all_gather | solution.py:17
  213.2 12.0 %multiply_reduce_fusion = (f32[512]{0:T(512)}, f32[512,256]{0,1:T(8,128)S(1)}) fusion(f32[512]{0:T(512)S(1)} %add_sqrt_fusion, bf16[512,256]{0,1:T(8,128)(2,1)S(1)} %copy.38, bf16[1,512,256]{1,2,0:T(8,128)(2,1)S(1)} %copy.33, bf16[1,8192,256]{2,1,0:T(8,128)(2,1)} %all-gather.10.cloned.1.call-done, bf16[512,256]{0,1:T(8,128)(2,1)S(1)} %copy-done.3, ...), kind=kOutput, calls=%fused_computation.83 | convolution fusion | flops 4325113344 | bytes 5611520 | tf_op jit(solution)/shard_map/qk,qd->kd/dot_general | solution.py:147
  226.9 3.1 scatter_custom_fusion.1
  230.0 34.2 %all_to_all.31 = bf16[16,4,32,256]{3,2,1,0:T(8,128)(2,1)S(1)} all-to-all(bf16[16,4,32,256]{3,2,1,0:T(8,128)(2,1)S(1)} %bitcast.221), channel_id=1, replica_groups=mesh['dp_0'=4,'dp_1'=4,'expert'=16] {'expert'}, dimensions={0} | all-to-all | bytes 2097152 | tf_op jit(solution)/shard_map/all_to_all | solution.py:151
  265.1 4.8 %fusion.34 = bf16[1024,4,256]{0,2,1:T(8,128)(2,1)} fusion(bf16[16,4,32,256]{3,2,1,0:T(8,128)(2,1)S(1)} %all_to_all.31, bf16[16,4,32,1024]{3,2,0,1:T(8,128)(2,1)} %copy-done.19), kind=kOutput, calls=%fused_computation.53 | convolution fusion | flops 1074790400 | bytes 7340032 | tf_op jit(solution)/shard_map/skcr,skcd->rkd/dot_general | solution.py:175
  270.0 4.0 copy.49
  274.0 3.2 copy.50
  277.2 6.3 %all-to-all-start.5 = ((bf16[16,64,4,256]{3,1,2,0:T(8,128)(2,1)}), bf16[16,64,4,256]{3,1,2,0:T(8,128)(2,1)}, u32[]{:S(2)}, u32[]{:S(2)}) async-start(bf16[16,64,4,256]{3,1,2,0:T(8,128)(2,1)} %copy.50), calls=%async_computation.5 | async-start | bytes 4194304 | tf_op jit(solution)/shard_map/all_to_all | solution.py:42
  283.5 9.2 %fusion.22 = bf16[16,4,32,1024]{3,2,0,1:T(8,128)(2,1)S(1)} fusion(f32[4,16,32,1024]{3,2,1,0:T(8,128)} %get-tuple-element.94, bf16[4,1024,256]{2,1,0:T(8,128)(2,1)} %param.13, bf16[16,4,32,256]{3,2,1,0:T(8,128)(2,1)S(1)} %copy-done.7), kind=kOutput, calls=%fused_computation.36 | convolution fusion | flops 1115684864 | bytes 15728640 | tf_op jit(solution)/shard_map/skcd,kfd->skcf/dot_general | solution.py:154
  294.6 1.6 copy.46
  296.2 17.9 %all-to-all-done.5 = bf16[16,64,4,256]{3,1,2,0:T(8,128)(2,1)} async-done(((bf16[16,64,4,256]{3,1,2,0:T(8,128)(2,1)}), bf16[16,64,4,256]{3,1,2,0:T(8,128)(2,1)}, u32[]{:S(2)}, u32[]{:S(2)}) %all-to-all-start.5) | async-done | bytes 2097184 | tf_op jit(solution)/shard_map/all_to_all | solution.py:42
  314.1 6.8 %all-to-all-start.4 = ((bf16[16,16,4,1024]{3,1,2,0:T(8,128)(2,1)}), bf16[16,16,4,1024]{3,1,2,0:T(8,128)(2,1)}, u32[]{:S(2)}, u32[]{:S(2)}) async-start(bf16[16,16,4,1024]{3,1,2,0:T(8,128)(2,1)} %copy.46), calls=%async_computation.4 | async-start | bytes 4194304 | tf_op jit(solution)/shard_map/all_to_all | solution.py:42
  320.9 6.4 %copy.39 = bf16[8192,256]{1,0:T(8,128)(2,1)} copy(bf16[8192,256]{0,1:T(8,128)(2,1)} %all-gather.6.cloned.1.call-done) | data formatting | bytes 8388608 | tf_op jit(solution)/shard_map/all_gather | solution.py:92
  327.3 3.5 fusion.50
  331.9 17.9 %all-to-all-done.4 = bf16[16,16,4,1024]{3,1,2,0:T(8,128)(2,1)} async-done(((bf16[16,16,4,1024]{3,1,2,0:T(8,128)(2,1)}), bf16[16,16,4,1024]{3,1,2,0:T(8,128)(2,1)}, u32[]{:S(2)}, u32[]{:S(2)}) %all-to-all-start.4) | async-done | bytes 2097184 | tf_op jit(solution)/shard_map/all_to_all | solution.py:42
  349.9 3.9 all-to-all-start.3
  353.8 57.2 %while.10 = (s32[]{:T(128)}, bf16[16,512,512]{1,2,0:T(8,128)(2,1)}, f32[1,512]{1,0:T(1,128)S(1)}, bf16[16,512,256]{2,1,0:T(8,128)(2,1)}, bf16[512,256]{1,0:T(8,1...) while((s32[]{:T(128)}, bf16[16,512,512]{1,2,0:T(8,128)(2,1)}, ...), condition=%wide.region_10.11_spmd, body=%wide.region_9.10_spmd.sunk | while | flops 136053248 | bytes 1066105 | solution.py:126
  355.1 2.3 fusion.98
  358.6 2.3 fusion.98
  362.2 2.3 fusion.98
  365.8 2.3 fusion.98
  369.4 2.3 fusion.98
  372.9 2.3 fusion.98
  376.5 2.3 fusion.98
  380.1 2.3 fusion.98
  383.7 2.3 fusion.98
  387.2 2.3 fusion.98
  390.8 2.3 fusion.98
  394.4 2.3 fusion.98
  398.0 2.3 fusion.98
  401.5 2.3 fusion.98
  405.1 2.3 fusion.98
  408.7 2.3 fusion.98
  411.6 7.7 %convolution_bitcast_fusion = f32[1,512,256]{2,1,0:T(8,128)} fusion(bf16[16,512,512]{1,2,0:T(8,128)(2,1)} %get-tuple-element.52, bf16[16,512,256]{2,1,0:T(8,128)(2,1)} %get-tuple-element.187), kind=kOutput, calls=%fused_computation.65 | convolution fusion | flops 2147483648 | bytes 13107200 | tf_op jit(solution)/shard_map/ira,ias->rs/dot_general | solution.py:129
  419.3 2.0 convert_reduce_fusion
  422.2 2.0 convert_reduce_fusion.1
  425.1 2.6 gather_fusion.1
  428.9 1.4 fusion.64
  (139 shorter events, 44.0 us)
Async XLA Ops:
  7.2 44.7 %copy-start = (bf16[4,256,1024]{2,1,0:T(8,128)(2,1)S(1)}, bf16[4,256,1024]{2,1,0:T(8,128)(2,1)}, u32[]{:S(2)}) copy-start(bf16[4,256,1024]{2,1,0:T(8,128)(2,1)} %param.12) | copy-start | bytes 6291460
  13.1 51.8 %copy-start.12 = (s32[512,1]{0,1:T(1,128)}, s32[512,1]{0,1:T(1,128)S(1)}, u32[]{:S(2)}) copy-start(s32[512,1]{0,1:T(1,128)S(1)} %compare_select_fusion) | copy-start | bytes 6148
  51.8 5.0 %copy-start.4 = (bf16[16,4,32,256]{3,2,1,0:T(8,128)(2,1)}, bf16[16,4,32,256]{3,2,1,0:T(8,128)(2,1)S(1)}, u32[]{:S(2)}) copy-start(bf16[16,4,32,256]{3,2,1,0:T(8,128)(2,1)S(1)} %all_to_all.30) | copy-start | bytes 3145732
  51.8 5.0 %copy-start.18 = (bf16[4,1024,256]{2,1,0:T(8,128)(2,1)S(1)}, bf16[4,1024,256]{2,1,0:T(8,128)(2,1)}, u32[]{:S(2)}) copy-start(bf16[4,1024,256]{2,1,0:T(8,128)(2,1)} %param.13) | copy-start | bytes 6291460
  56.8 2.0 copy-start.19
  56.8 39.9 %copy-start.8 = (s32[1,8192]{1,0:T(1,128)S(1)}, s32[1,8192]{1,0:T(1,128)}, u32[]{:S(2)}) copy-start(s32[1,8192]{1,0:T(1,128)} %param.17) | copy-start | bytes 98308
  56.8 40.5 %copy-start.13 = (s32[1,512]{1,0:T(1,128)S(1)}, s32[1,512]{1,0:T(1,128)}, u32[]{:S(2)}) copy-start(s32[1,512]{1,0:T(1,128)} %param.16) | copy-start | bytes 6148
  59.9 30.8 %all-to-all-start.1 = ((bf16[16,4,32,256]{3,2,1,0:T(8,128)(2,1)}), bf16[16,4,32,256]{3,2,1,0:T(8,128)(2,1)S(1)}, u32[]{:S(2)}, u32[]{:S(2)}) async-start(bf16[16,4,32,256]{3,2,1,0:T(8,128)(2,1)} %copy.37), calls=%async_computation.1 | async-start | bytes 2097152 | tf_op jit(solution)/shard_map/all_to_all | solution.py:82
  64.1 31.3 %all-gather.8.cloned.1.call-start = ((), (), s32[]{:S(2)}) async-start(), calls=%async_computation.7 | async-start | bytes 1310720 | tf_op jit(solution)/shard_map/all_gather | solution.py:17
  64.8 95.4 %all-gather.6.cloned.1.call-start = ((), (), s32[]{:S(2)}) async-start(), calls=%async_computation.6 | async-start | bytes 4456448 | tf_op jit(solution)/shard_map/all_gather | solution.py:92
  64.9 31.2 %copy-start.9 = (s32[1024]{0:T(1024)}, s32[1024]{0:T(1024)S(1)}, u32[]{:S(2)}) copy-start(s32[1024]{0:T(1024)S(1)} %pad_clamp_fusion) | copy-start | bytes 12292
  94.4 130.8 %copy-start.1 = (bf16[512,256]{0,1:T(8,128)(2,1)}, bf16[512,256]{0,1:T(8,128)(2,1)S(1)}, u32[]{:S(2)}) copy-start(bf16[512,256]{0,1:T(8,128)(2,1)S(1)} %copy.38) | copy-start | bytes 786436
  95.3 117.9 %all-gather.10.cloned.1.call-start = ((), (), s32[]{:S(2)}) async-start(), calls=%async_computation.8 | async-start | bytes 5242880 | tf_op jit(solution)/shard_map/all_gather | solution.py:17
  165.6 5.4 %copy-start.16 = (f32[1,512]{1,0:T(1,128)S(1)}, f32[1,512]{1,0:T(1,128)}, u32[]{:S(2)}) copy-start(f32[1,512]{1,0:T(1,128)} %param.15) | copy-start | bytes 6148
  165.7 47.6 %copy-start.3 = (bf16[512,256]{0,1:T(8,128)(2,1)S(1)}, bf16[512,256]{0,1:T(8,128)(2,1)}, u32[]{:S(2)}) copy-start(bf16[512,256]{0,1:T(8,128)(2,1)} %fusion.80) | copy-start | bytes 786436
  225.2 0.8 copy-start.2
  264.2 1.0 copy-start.6
  270.0 13.5 %copy-start.7 = (bf16[16,4,32,256]{3,2,1,0:T(8,128)(2,1)S(1)}, bf16[16,4,32,256]{3,2,1,0:T(8,128)(2,1)}, u32[]{:S(2)}) copy-start(bf16[16,4,32,256]{3,2,1,0:T(8,128)(2,1)} %copy-done.6) | copy-start | bytes 3145732
  277.2 36.8 %all-to-all-start.5 = ((bf16[16,64,4,256]{3,1,2,0:T(8,128)(2,1)}), bf16[16,64,4,256]{3,1,2,0:T(8,128)(2,1)}, u32[]{:S(2)}, u32[]{:S(2)}) async-start(bf16[16,64,4,256]{3,1,2,0:T(8,128)(2,1)} %copy.50), calls=%async_computation.5 | async-start | bytes 4194304 | tf_op jit(solution)/shard_map/all_to_all | solution.py:42
  283.5 9.2 %copy-start.5 = (bf16[16,4,32,256]{3,2,1,0:T(8,128)(2,1)S(1)}, bf16[16,4,32,256]{3,2,1,0:T(8,128)(2,1)}, u32[]{:S(2)}) copy-start(bf16[16,4,32,256]{3,2,1,0:T(8,128)(2,1)} %copy-done.4) | copy-start | bytes 3145732
  292.7 1.9 copy-start.20
  314.1 35.8 %all-to-all-start.4 = ((bf16[16,16,4,1024]{3,1,2,0:T(8,128)(2,1)}), bf16[16,16,4,1024]{3,1,2,0:T(8,128)(2,1)}, u32[]{:S(2)}, u32[]{:S(2)}) async-start(bf16[16,16,4,1024]{3,1,2,0:T(8,128)(2,1)} %copy.46), calls=%async_computation.4 | async-start | bytes 4194304 | tf_op jit(solution)/shard_map/all_to_all | solution.py:42
  327.2 26.5 %copy-start.14 = (s32[1,512]{1,0:T(1,128)S(1)}, s32[1,512]{1,0:T(1,128)}, u32[]{:S(2)}) copy-start(s32[1,512]{1,0:T(1,128)} %param.16) | copy-start | bytes 6148
  327.2 26.6 %copy-start.17 = (f32[1,512]{1,0:T(1,128)S(1)}, f32[1,512]{1,0:T(1,128)}, u32[]{:S(2)}) copy-start(f32[1,512]{1,0:T(1,128)} %param.15) | copy-start | bytes 6148
  330.8 80.2 %copy-start.15 = (f32[512]{0:T(512)S(1)}, f32[512]{0:T(512)}, u32[]{:S(2)}) copy-start(f32[512]{0:T(512)} %get-tuple-element.69) | copy-start | bytes 6148
  349.9 75.2 %all-to-all-start.3 = ((bf16[16,4,32,256]{3,2,1,0:T(8,128)(2,1)}), bf16[16,4,32,256]{3,2,1,0:T(8,128)(2,1)S(1)}, u32[]{:S(2)}, u32[]{:S(2)}) async-start(bf16[16,4,32,256]{3,2,1,0:T(8,128)(2,1)} %copy.43), calls=%async_computation.3 | async-start | bytes 2097152 | tf_op jit(solution)/shard_map/all_to_all | solution.py:161
  411.6 13.5 %copy-start.10 = (s32[1024]{0:T(1024)S(1)}, s32[1024]{0:T(1024)}, u32[]{:S(2)}) copy-start(s32[1024]{0:T(1024)} %copy-done.9) | copy-start | bytes 12292
  419.3 9.6 %copy-start.11 = (f32[512]{0:T(512)S(1)}, f32[512]{0:T(512)}, u32[]{:S(2)}) copy-start(f32[512]{0:T(512)} %get-tuple-element.97) | copy-start | bytes 6148
Sparse Core Ops, SparseCore 0:
  66.7 26.5 all-gather.7
  96.3 63.8 all-gather.5
  162.0 51.1 all-gather.9
where the time goes:
time: 442 us; the launch traced here: 438 us
  waiting for transfers between devices  146 us (33%)
  blocking collectives  91.6 us (21%)
  matrix products  87.2 us (20%)
  local copies, waits for them, and re-layouts  49.3 us (11%)
  other arithmetic  27.9 us (6%)
  starting transfers between devices  21.3 us (5%)
  between operations  14.1 us (3%)
    all_gather x1, waiting for transfers between devices, per_device(): shard_rows = lax.all_gather(unit_low, DP, axis=0, tiled=True)  62.8 us
    dot_general x16, matrix products, weigh_block(): jnp.einsum('qd,kd->qk', query_matrix, item_tile_rows, preferred_element_t...  37 us
    all_to_all x2, waiting for transfers between devices, sum_at_owner(): lax.all_to_all(in_blocks(shard, dim, peers), axis, 0, 0, tiled=True)  35.8 us
    all_to_all x1, blocking collectives, per_device(): lax.all_to_all(scatter_slots(normed), 'expert', split_axis=0, concat_axis...  35.6 us
    all_to_all x1, blocking collectives, per_device(): lax.all_to_all(scatter_slots(grad_low), 'expert', split_axis=0, concat_ax...  34.2 us
    all_to_all x1, waiting for transfers between devices, per_device(): lax.all_to_all(output, 'expert', split_axis=0, concat_axis=0, tiled=True)  25.8 us
    all_gather x1, blocking collectives, turned_gather(): whole = lax.all_gather(both, axis, axis=0, tiled=True)  21.8 us
    all_gather x2, waiting for transfers between devices, whole_of(): whole = lax.all_gather(whole, axes[number], axis=dim, tiled=True)  20.3 us
  transfers between devices with their start and end apart: 7, of which 5 were waited for; matrix products, arithmetic and copies ran while one was open for 25% of the time, Pallas kernels for 0%

commit v1 on v0

v1 whole, which is shorter than its diff:
```python
import functools
import math

import jax
import jax.numpy as jnp
from jax import lax
from jax.experimental import pallas as pl
from jax.experimental.pallas import tpu as pltpu
from jax.sharding import Mesh
from jax.sharding import PartitionSpec as P

AXES = ("x", "y", "z", "c")
SIZE = {"x": 4, "y": 4, "z": 8, "c": 2}
N = 512
D = 256
FF = 1024
NE = 4
CAP = 32
EXPERTS = 64
GROUP = 16
SLOTS = NE * CAP
EPS = 1e-6
K0 = math.sqrt(2.0 / math.pi)
K1 = K0 * 0.044715
BF = jnp.bfloat16
F32 = jnp.float32

DZ = (0, 1, 7, 2, 6, 3, 5, 4)


def at(axis, step):
    return lax.rem(lax.axis_index(axis) + (step % SIZE[axis]), SIZE[axis])


def z_peer(p, sign):
    return {"z": at("z", sign * DZ[p // 2]), "c": at("c", p % 2)}


def xy_peer(j):
    return {"x": at("x", j // 4), "y": at("y", j % 4)}


def nt(a, b):
    return lax.dot_general(a, b, (((1,), (1,)), ((), ())), preferred_element_type=F32)


def nn(a, b):
    return jnp.dot(a, b, preferred_element_type=F32)


def remote(src, dst, send, recv, peer):
    return pltpu.make_async_remote_copy(
        src_ref=src, dst_ref=dst, send_sem=send, recv_sem=recv, device_id=peer
    )


class RingGather:
    def __init__(self, buf, send, recv):
        self.buf, self.send, self.recv = buf, send, recv
        self.copies = {}

    def go(self, number, view, peer):
        c = remote(view, view, self.send.at[number], self.recv.at[number], peer)
        c.start()
        self.copies[number] = c

    def got(self, *numbers):
        for n in numbers:
            self.copies[n].wait_recv()

    def step(self, s):
        buf, h, q = self.buf, N // 2, N // 4
        x, y = lax.axis_index("x"), lax.axis_index("y")
        xl, xr, yl, yr = at("x", -1), at("x", 1), at("y", -1), at("y", 1)
        top, bot = pl.ds(0, h), pl.ds(h, h)
        parts = [pl.ds(i * q, q) for i in range(4)]
        if s == 0:
            self.go(0, buf.at[x, y, top], {"x": xr})
            self.go(1, buf.at[x, y, top], {"x": xl})
            self.go(2, buf.at[x, y, bot], {"y": yr})
            self.go(3, buf.at[x, y, bot], {"y": yl})
        elif s == 1:
            self.got(0, 1, 2, 3)
            self.go(4, buf.at[xl, y, parts[0]], {"x": xr})
            self.go(5, buf.at[xr, y, parts[1]], {"x": xl})
            self.go(6, buf.at[x, yl, parts[2]], {"y": yr})
            self.go(7, buf.at[x, yr, parts[3]], {"y": yl})
        elif s == 2:
            self.got(4, 5, 6, 7)
            self.go(8, buf.at[:, y, top], {"y": yr})
            self.go(9, buf.at[:, y, top], {"y": yl})
            self.go(10, buf.at[x, :, bot], {"x": xr})
            self.go(11, buf.at[x, :, bot], {"x": xl})
        elif s == 3:
            self.got(8, 9, 10, 11)
            self.go(12, buf.at[:, yl, parts[0]], {"y": yr})
            self.go(13, buf.at[:, yr, parts[1]], {"y": yl})
            self.go(14, buf.at[xl, :, parts[2]], {"x": xr})
            self.go(15, buf.at[xr, :, parts[3]], {"x": xl})
        else:
            self.got(12, 13, 14, 15)
            for c in self.copies.values():
                c.wait_send()


def kernel(
    feats, ids_col, ids_row, w_in_hbm, w_out_hbm, queries, qw_row, pos_row, qw_col, pos_col, logc_col, logc_all,
    loss_o, gq_o, gi_o, gwi_o, gwo_o,
    w_in, w_out, q_all, u_all, nrm, ulow, unit, invlen, gs, acc, lb, plr, plc,
    snd, rcv, outb, ret, gsnd, grcv, gnb, gnret,
    gp, act_t, x_t, gh, pin, pout, ra_in, ra_out, pa_in, pa_out, rb_in, rb_out,
    st_s, st_r, bc_s, bc_r,
    loc_sem, a1s, a1r, a2s, a2r, a3s, a3r, a4s, a4r, qs, qr, us, ur, sts, str_, bcs, bcr, rs_s, rs_r,
):
    x, y, z, c = (lax.axis_index(a) for a in AXES)
    barrier = pltpu.get_barrier_semaphore()
    for p in range(1, GROUP):
        pl.semaphore_signal(barrier, inc=1, device_id=z_peer(p, 1))
    for j in range(1, GROUP):
        pl.semaphore_signal(barrier, inc=1, device_id=xy_peer(j))

    load_in = pltpu.make_async_copy(w_in_hbm, w_in, loc_sem.at[0])
    load_out = pltpu.make_async_copy(w_out_hbm, w_out, loc_sem.at[1])
    load_in.start()
    load_out.start()
    q_all[x, y] = queries[...]

    def place(ids, rank):
        owner = ids >> 2
        dz = ((owner >> 1) - z) & 7
        dc = ((owner & 1) - c) & 1
        pz = jnp.where(dz <= 4, jnp.maximum(2 * dz - 1, 0), 16 - 2 * dz)
        return (pz * 2 + dc) * SLOTS + (ids & 3) * CAP + rank

    f = feats[...].astype(F32)
    r = lax.rsqrt(jnp.mean(f * f, axis=1, keepdims=True) + EPS)
    nrm[...] = (f * r).astype(BF)
    row_i = lax.broadcasted_iota(jnp.int32, (N, N), 0)
    col_i = lax.broadcasted_iota(jnp.int32, (N, N), 1)
    idr = ids_row[...]
    hot_r = lax.broadcasted_iota(jnp.int32, (EXPERTS, N), 0) == idr
    before = nn(hot_r.astype(F32).astype(BF), (row_i < col_i).astype(F32).astype(BF))
    rank_r = jnp.sum(jnp.where(hot_r, before, 0.0), axis=0, keepdims=True)
    plr[...] = place(idr, rank_r.astype(jnp.int32))
    idc = ids_col[...]
    hot_c = lax.broadcasted_iota(jnp.int32, (N, EXPERTS), 1) == idc
    before = nn((row_i > col_i).astype(F32).astype(BF), hot_c.astype(F32).astype(BF))
    rank_c = jnp.sum(jnp.where(hot_c, before, 0.0), axis=1, keepdims=True)
    plc[...] = jnp.broadcast_to(place(idc, rank_c.astype(jnp.int32)), (N, 2 * SLOTS))
    lb[...] = jnp.broadcast_to(logc_col[...], (N, D))

    def packed(values, p):
        slot = lax.broadcasted_iota(jnp.int32, (SLOTS, N), 0) + p * SLOTS
        pick = (slot == plr[...]).astype(F32).astype(BF)
        return nn(pick, values[...]).astype(BF).reshape(NE, CAP, D)

    def unpacked(source, i):
        slot = lax.broadcasted_iota(jnp.int32, (N, 2 * SLOTS), 1) + i * 2 * SLOTS
        pick = (slot == plc[...]).astype(F32).astype(BF)
        return nn(pick, source[pl.ds(2 * i, 2)].reshape(2 * SLOTS, D))

    pl.semaphore_wait(barrier, 2 * (GROUP - 1))
    gather_q = RingGather(q_all, qs, qr)
    gather_q.step(0)

    def dispatch(values, out, into, send, recv):
        copies = {}
        for p in range(GROUP):
            if p == 0:
                into[0] = packed(values, 0)
            else:
                out[p] = packed(values, p)
                copies[p] = remote(out.at[p], into.at[p], send.at[p], recv.at[p], z_peer(p, 1))
                copies[p].start()
        return copies

    def give_back(out, into, send, recv, p):
        copy = remote(out.at[p], into.at[p], send.at[p], recv.at[p], z_peer(p, -1))
        copy.start()
        return copy

    sent1 = dispatch(nrm, snd, rcv, a1s, a1r)
    load_in.wait()
    load_out.wait()
    gather_q.step(1)

    back2 = {}
    for b in range(4):
        for p in range(4 * b, 4 * b + 4):
            if p:
                sent1[p].wait_recv()

        def forward(e, _, b=b):
            rows = rcv[pl.ds(4 * b, 4), e].reshape(4 * CAP, D)
            h = nn(rows, w_in[e])
            gp[b, e] = h
            t = jnp.tanh(h * (K0 + K1 * (h * h)))
            act = (h * (0.5 + 0.5 * t)).astype(BF)
            out = nn(act, w_out[e]).astype(BF)
            outb[pl.ds(4 * b, 4), e] = out.reshape(4, CAP, D)
            return _

        lax.fori_loop(0, NE, forward, 0)
        for p in range(4 * b, 4 * b + 4):
            if p:
                back2[p] = give_back(outb, ret, a2s, a2r, p)
        if b == 0:
            ret[0] = outb[0]
        if b < 3:
            gather_q.step(2 + b)

    for b in range(4):

        def keep(e, _, b=b):
            h = gp[b, e]
            u = h * h
            t = jnp.tanh(h * (K0 + K1 * u))
            cdf = 0.5 + 0.5 * t
            act = (h * cdf).astype(BF)
            gp[b, e] = cdf + (0.5 * h) * (1.0 - t * t) * (K0 + (3.0 * K1) * u)
            act_t[e, :, pl.ds(4 * CAP * b, 4 * CAP)] = act.T
            rows = rcv[pl.ds(4 * b, 4), e].reshape(4 * CAP, D)
            x_t[e, :, pl.ds(4 * CAP * b, 4 * CAP)] = rows.T
            return _

        lax.fori_loop(0, NE, keep, 0)

    acc[...] = jnp.zeros((N, D), F32)
    for i in range(8):
        for p in (2 * i, 2 * i + 1):
            if p:
                back2[p].wait_recv()
        acc[...] += unpacked(ret, i)

    summed = feats[...].astype(F32) + acc[...]
    length = jnp.sqrt(jnp.sum(summed * summed, axis=1, keepdims=True) + EPS)
    inv = 1.0 / length
    un = summed * inv
    unit[...] = un
    invlen[...] = jnp.broadcast_to(inv, (N, 128))
    ulow[...] = un.astype(BF)
    u_all[x, y] = un.astype(BF)
    gather_u = RingGather(u_all, us, ur)
    gather_u.step(0)

    T = 256

    def scores(qx, qy, t):
        return nt(ulow[...], q_all[qx, qy, pl.ds(t * T, T)]) - lb[...]

    def stat_block(j, _):
        qx, qy = lax.rem(x + j // 4, 4), lax.rem(y + lax.rem(j, 4), 4)
        for t in range(N // T):
            s = scores(qx, qy, t)
            m = jnp.max(s, axis=0, keepdims=True)
            st_s[j, 0:1, pl.ds(t * T, T)] = m
            st_s[j, 1:2, pl.ds(t * T, T)] = jnp.sum(jnp.exp(s - m), axis=0, keepdims=True)
        return _

    st_copies = {}
    for part in range(4):
        lax.fori_loop(4 * part, 4 * part + 4, stat_block, 0)
        for j in range(4 * part, 4 * part + 4):
            if j:
                st_copies[j] = remote(st_s.at[j], st_r.at[j], sts.at[j], str_.at[j], xy_peer(j))
                st_copies[j].start()
        if part < 3:
            gather_u.step(1 + part)
    st_r[0] = st_s[0]
    for j in range(1, GROUP):
        st_copies[j].wait_recv()
    top = jnp.max(st_r[:, 0:1, :], axis=0)
    total = jnp.sum(st_r[:, 1:2, :] * jnp.exp(st_r[:, 0:1, :] - top[None]), axis=0)
    lse = top + jnp.log(total)
    shift = lse - jnp.log(qw_row[...])
    bc_s[0:1] = shift
    bc_s[1:2] = qw_row[...]
    bc_s[2:3] = pos_row[...].astype(F32)
    bc_s[3:4] = lse
    bc_copies = {}
    for j in range(1, GROUP):
        bc_copies[j] = remote(bc_s, bc_r.at[j], bcs.at[j], bcr.at[j], xy_peer(j))
        bc_copies[j].start()
    bc_r[0] = bc_s[...]
    first_item = ((x * 4 + y) * N).astype(F32)

    acc[...] = jnp.zeros((N, D), F32)
    item_row = lax.broadcasted_iota(jnp.int32, (N, T), 0)

    def grad_block(j, _):
        qx, qy = lax.rem(x + 4 - j // 4, 4), lax.rem(y + 4 - lax.rem(j, 4), 4)
        for t in range(N // T):
            span = pl.ds(t * T, T)
            s = scores(qx, qy, t)
            e = jnp.exp(s - bc_r[j, 0:1, span])
            own = (bc_r[j, 2:3, span] - first_item).astype(jnp.int32)
            coeff = (e - jnp.where(item_row == own, bc_r[j, 1:2, span], 0.0)).astype(BF)
            acc[...] += nn(coeff, q_all[qx, qy, span])
        return _

    for part in range(4):
        for j in range(4 * part, 4 * part + 4):
            if j:
                bc_copies[j].wait_recv()
        lax.fori_loop(4 * part, 4 * part + 4, grad_block, 0)

    g = acc[...]
    un = unit[...]
    along = jnp.sum(un * g, axis=1, keepdims=True)
    gsum = (g - un * along) * invlen[:, 0:1]
    gs[...] = gsum
    nrm[...] = gsum.astype(BF)
    sent3 = dispatch(nrm, gsnd, grcv, a3s, a3r)
    gather_u.step(4)

    acc[...] = jnp.zeros((N, D), F32)
    lse_c = jnp.transpose(jnp.broadcast_to(lse, (8, N)))[:, 0:1]
    shift_c = lse_c - jnp.log(qw_col[...])
    lb[...] = jnp.broadcast_to(shift_c, (N, D))
    plq = jnp.broadcast_to(pos_col[...], (N, 128))
    invlen[...] = jnp.zeros((N, 128), F32)

    def query_block(d, _):
        ix, iy = d // 4, lax.rem(d, 4)
        for t in range(N // 128):
            span = pl.ds(t * 128, 128)
            s = nt(queries[...], u_all[ix, iy, span]) - logc_all[d, 0:1, span]
            e = jnp.exp(s - lb[:, 0:128])
            hit = lax.broadcasted_iota(jnp.int32, (N, 128), 1) + (d * N + t * 128) == plq
            coeff = (e - jnp.where(hit, jnp.broadcast_to(qw_col[...], (N, 128)), 0.0)).astype(BF)
            invlen[...] += jnp.where(hit, s, 0.0)
            acc[...] += nn(coeff, u_all[ix, iy, span])
        return _

    lax.fori_loop(0, GROUP, query_block, 0)
    gq_o[...] = acc[...]
    picked = jnp.sum(invlen[...], axis=1, keepdims=True)
    loss_c = jnp.broadcast_to(lse_c - picked, (N, 128))
    loss_o[...] = jnp.transpose(loss_c)[0:1]

    back4 = {}
    for b in range(4):
        for p in range(4 * b, 4 * b + 4):
            if p:
                sent3[p].wait_recv()

        def backward(e, _, b=b):
            rows = grcv[pl.ds(4 * b, 4), e].reshape(4 * CAP, D)
            ga = nt(rows, w_out[e])
            ghv = (ga * gp[b, e]).astype(BF)
            gh[e, pl.ds(4 * CAP * b, 4 * CAP)] = ghv
            gnb[pl.ds(4 * b, 4), e] = nt(ghv, w_in[e]).astype(BF).reshape(4, CAP, D)
            return _

        lax.fori_loop(0, NE, backward, 0)
        for p in range(4 * b, 4 * b + 4):
            if p:
                back4[p] = give_back(gnb, gnret, a4s, a4r, p)
        if b == 0:
            gnret[0] = gnb[0]

    def weights(e, _):
        pin[:, :, e] = nn(x_t[e], gh[e]).astype(BF).reshape(4, 4, 16, FF)
        rows = grcv[:, e].reshape(GROUP * CAP, D)
        pout[:, :, e] = nn(act_t[e], rows).astype(BF).reshape(4, 4, 64, D)
        return _

    lax.fori_loop(0, NE, weights, 0)

    rs = {}

    def rs_go(number, src, dst, peer):
        rs[number] = remote(src, dst, rs_s.at[number], rs_r.at[number], peer)
        rs[number].start()

    for k in (1, 3, 2):
        rs_go(k - 1, pin.at[at("x", k)], ra_in.at[k - 1], {"x": at("x", k)})
        rs_go(k + 2, pout.at[:, at("y", k)], ra_out.at[k - 1], {"y": at("y", k)})

    acc[...] = jnp.zeros((N, D), F32)
    for i in range(8):
        for p in (2 * i, 2 * i + 1):
            if p:
                back4[p].wait_recv()
        acc[...] += unpacked(gnret, i)
    f = feats[...].astype(F32)
    r = lax.rsqrt(jnp.mean(f * f, axis=1, keepdims=True) + EPS)
    grows = acc[...]
    projected = jnp.mean(grows * f, axis=1, keepdims=True)
    gi_o[...] = gs[...] + r * (grows - f * (r * r * projected))

    for n in range(6):
        rs[n].wait_recv()
    for k in range(4):
        t = pin[x, k].astype(F32)
        u = pout[k, y].astype(F32)
        for i in range(3):
            t = t + ra_in[i, k].astype(F32)
            u = u + ra_out[i, k].astype(F32)
        pa_in[k] = t.astype(BF)
        pa_out[k] = u.astype(BF)
    for k in (1, 3, 2):
        rs_go(k + 5, pa_in.at[at("y", k)], rb_in.at[k - 1], {"y": at("y", k)})
        rs_go(k + 8, pa_out.at[at("x", k)], rb_out.at[k - 1], {"x": at("x", k)})
    for n in range(6, 12):
        rs[n].wait_recv()
    t = pa_in[y].astype(F32)
    u = pa_out[x].astype(F32)
    for i in range(3):
        t = t + rb_in[i].astype(F32)
        u = u + rb_out[i].astype(F32)
    gwi_o[...] = t
    gwo_o[...] = u

    for group in (sent1, back2, sent3, back4, st_copies, bc_copies, rs):
        for copy in group.values():
            copy.wait_send()


def per_device(feats, ids, w_in, w_out, queries, qw, pos, counts):
    d = lax.axis_index("x") * 4 + lax.axis_index("y")
    logc = jnp.log(counts[0].astype(F32)).reshape(GROUP, 1, N)
    own = lax.dynamic_index_in_dim(logc, d, 0, keepdims=False).reshape(N, 1)
    vm = pl.BlockSpec(memory_space=pltpu.VMEM)
    hbm = pl.BlockSpec(memory_space=pl.ANY)
    V = pltpu.VMEM
    sem = pltpu.SemaphoreType.DMA
    slots = (GROUP, NE, CAP, D)
    scratch = [
        V((NE, D, FF), BF), V((NE, FF, D), BF), V((4, 4, N, D), BF), V((4, 4, N, D), BF),
        V((N, D), BF), V((N, D), BF), V((N, D), F32), V((N, 128), F32), V((N, D), F32), V((N, D), F32), V((N, D), F32),
        V((1, N), jnp.int32), V((N, 2 * SLOTS), jnp.int32),
        *[V(slots, BF) for _ in range(8)],
        V((4, NE, 4 * CAP, FF), F32), V((NE, FF, N), BF), V((NE, D, N), BF), V((NE, N, FF), BF),
        V((4, 4, NE, 16, FF), BF), V((4, 4, NE, 64, D), BF),
        V((3, 4, NE, 16, FF), BF), V((3, 4, NE, 64, D), BF),
        V((4, NE, 16, FF), BF), V((4, NE, 64, D), BF),
        V((3, NE, 16, FF), BF), V((3, NE, 64, D), BF),
        V((GROUP, 2, N), F32), V((GROUP, 2, N), F32), V((4, N), F32), V((GROUP, 4, N), F32),
        sem((2,)), *[sem((GROUP,)) for _ in range(16)], sem((12,)), sem((12,)),
    ]
    outs = (
        jax.ShapeDtypeStruct((1, N), F32),
        jax.ShapeDtypeStruct((N, D), F32),
        jax.ShapeDtypeStruct((N, D), F32),
        jax.ShapeDtypeStruct((NE, 16, FF), F32),
        jax.ShapeDtypeStruct((NE, 64, D), F32),
    )
    loss, gq, gi, gwi, gwo = pl.pallas_call(
        kernel,
        out_shape=outs,
        in_specs=[vm, vm, vm, hbm, hbm, vm, vm, vm, vm, vm, vm, vm],
        out_specs=[vm] * 5,
        scratch_shapes=scratch,
        compiler_params=pltpu.CompilerParams(
            collective_id=0, has_side_effects=True, vmem_limit_bytes=60 << 20
        ),
        name="tower_step",
    )(
        feats[0], ids[0], ids.reshape(1, N), w_in, w_out, queries[0], qw, pos,
        qw.reshape(N, 1), pos.reshape(N, 1), own, logc,
    )
    return (loss, gq[None], gi[None], jnp.transpose(gwi, (1, 0, 2)), jnp.transpose(gwo, (1, 0, 2)))


def solution(mesh):
    torus = Mesh(mesh.devices.reshape(4, 4, 8, 2), AXES)
    dp, ex = ("x", "y"), ("z", "c")
    in_specs = (
        P(ex, dp, None), P(ex, dp, None), P(ex, None, None), P(ex, None, None),
        P(ex, dp, None), P(ex, dp), P(ex, dp), P(ex, None),
    )
    out_specs = (
        P(ex, dp), P(ex, dp, None), P(ex, dp, None), P(dp, ex, None), P(dp, ex, None),
    )
    return jax.shard_map(
        per_device, mesh=torus, in_specs=in_specs, out_specs=out_specs, check_vma=False
    )
```

time: 442 us -> 188 us (0.43)
  Pallas kernels: 0 us -> 173 us
  waiting for transfers between devices: 146 us -> 0 us
  blocking collectives: 91.6 us -> 0 us
  matrix products: 87.2 us -> 0 us
  local copies, waits for them, and re-layouts: 49.3 us -> 13.1 us
  other arithmetic: 27.9 us -> 0.8 us
  starting transfers between devices: 21.3 us -> 0 us
  between operations: 14.1 us -> 0.68 us
    pallas_call x0 -> x1, Pallas kernels: none -> 173 us  [per_device(): pl.pallas_call(kernel, out_shape=outs, in_specs=[vm, vm, vm, hbm, hbm, vm...]
    dot_general x25 -> x0, matrix products: 87.2 us -> none  [the longest x16 37 us: weigh_block(): jnp.einsum('qd,kd->qk', query_matrix, item_tile_rows, preferred_element_t...]
    all_gather x3 -> x0, waiting for transfers between devices: 83.1 us -> none  [the longest x1 62.8 us: per_device(): shard_rows = lax.all_gather(unit_low, DP, axis=0, tiled=True)]
    all_to_all x2 -> x0, blocking collectives: 69.8 us -> none  [the longest x1 35.6 us: per_device(): lax.all_to_all(scatter_slots(normed), 'expert', split_axis=0, concat_axis...]
    all_to_all x4 -> x0, waiting for transfers between devices: 61.7 us -> none  [the longest x2 35.8 us: sum_at_owner(): lax.all_to_all(in_blocks(shard, dim, peers), axis, 0, 0, tiled=True)]
    all_gather x1 -> x0, blocking collectives: 21.8 us -> none  [turned_gather(): whole = lax.all_gather(both, axis, axis=0, tiled=True)]
    all_to_all x4 -> x0, starting transfers between devices: 21.2 us -> none  [the longest x2 13 us: sum_at_owner(): lax.all_to_all(in_blocks(shard, dim, peers), axis, 0, 0, tiled=True)]
    add x19 -> x0, other arithmetic: 11 us -> none  [the longest x16 10.3 us: weigh_block(): columns = first_item + jnp.arange(item_rows, dtype=jnp.int32)]
  transfers between devices with their start and end apart: 7 -> 0, of which waited for: 5 -> 0; matrix products, arithmetic and copies ran while one was open for 25% -> 0% of each run, Pallas kernels for 0% -> 0%
where the time goes in v1:
time: 188 us
  Pallas kernels  173 us (92%)
  local copies, waits for them, and re-layouts  13.1 us (7%)
    pallas_call x1, Pallas kernels, per_device(): pl.pallas_call(kernel, out_shape=outs, in_specs=[vm, vm, vm, hbm, hbm, vm...  173 us
    unnamed x9, local copies, waits for them, and re-layouts  7.63 us

profile of v1, /device:TPU:24, one launch (start us, length us, event | category | flops | bytes accessed | tf_op | source)
XLA Modules:
  0.0 187.7 jit_solution(76701669926214942)
XLA Ops:
  0.6 0.8 convert_log_fusion
  1.4 0.0 copy-start.1
  1.5 0.9 copy.18.logc_col
  2.3 1.5 copy.17.pos_col
  3.9 1.5 copy.16.qw_col
  5.4 1.5 copy.15.ids_col
  6.9 0.0 copy-done.1
  6.9 173.2 %tower_step.1 = (f32[1,512]{1,0:T(1,128)}, f32[512,256]{1,0:T(8,128)}, f32[512,256]{1,0:T(8,128)}, f32[4,16,1024]{2,1,0:T(8,128)}, f32[4,64,256]{2,1,0:T(8,128)}) custom-call(bf16[512,256]{1,0:T(8,128)(2,1)} %bitcast.15, s32[512,1]{1,0:T(8,128)} %copy.15.ids_col, s32[1,512]{1,0:T(1,128)} %bitcast.22, bf16[4,256,1024]{2,1,0:T(8,128)(2,1)} %w_in_hbm.1, ...), custom_call_target="tpu_custom_call" | custom-call | tf_op jit(solution)/shard_map/tower_step/pallas_call | solution.py:449
  180.1 0.0 copy-start
  180.1 1.9 %copy.19 = f32[16,4,1024]{2,1,0:T(4,128)} copy(f32[16,4,1024]{2,0,1:T(8,128)} %bitcast.18) | data formatting | bytes 524288
  182.0 1.8 copy.20
  183.8 1.3 copy.24
  185.1 1.9 copy.25
  186.9 0.0 copy-done
  186.9 0.8 copy.26
  (1 shorter events, 0.0 us)
Async XLA Ops:
  1.4 5.5 %copy-start.1 = (f32[1,8192]{1,0:T(1,128)}, f32[1,8192]{1,0:T(1,128)S(1)}, u32[]{:S(2)}) copy-start(f32[1,8192]{1,0:T(1,128)S(1)} %convert_log_fusion) | copy-start | bytes 98308
  180.1 6.8 %copy-start = (f32[512,256]{1,0:T(8,128)S(1)}, f32[512,256]{1,0:T(8,128)}, u32[]{:S(2)}) copy-start(f32[512,256]{1,0:T(8,128)} %get-tuple-element.12) | copy-start | bytes 1572868

commit v2 on v1

v2 whole, which is shorter than its diff:
```python
import functools
import math

import jax
import jax.numpy as jnp
from jax import lax
from jax.experimental import pallas as pl
from jax.experimental.pallas import tpu as pltpu
from jax.sharding import Mesh
from jax.sharding import PartitionSpec as P

AXES = ("x", "y", "z", "c")
SIZE = {"x": 4, "y": 4, "z": 8, "c": 2}
N = 512
D = 256
FF = 1024
NE = 4
CAP = 32
EXPERTS = 64
GROUP = 16
SLOTS = NE * CAP
NG = 2
EG = NE // NG
MSG = EG * CAP
GSLOTS = GROUP * MSG
T = 256
QCUT = 8
PACK = 512
EPS = 1e-6
K0 = math.sqrt(2.0 / math.pi)
K1 = K0 * 0.044715
BF = jnp.bfloat16
F32 = jnp.float32

DZ = (0, 1, 7, 2, 6, 3, 5, 4)


def at(axis, step):
    return lax.rem(lax.axis_index(axis) + (step % SIZE[axis]), SIZE[axis])


def z_peer(p, sign):
    return {"z": at("z", sign * DZ[p // 2]), "c": at("c", p % 2)}


def xy_peer(j):
    return {"x": at("x", j // 4), "y": at("y", j % 4)}


def nt(a, b):
    return lax.dot_general(a, b, (((1,), (1,)), ((), ())), preferred_element_type=F32)


def nn(a, b):
    return jnp.dot(a, b, preferred_element_type=F32)


class RingGather:
    def __init__(self, buf, send, recv):
        self.buf, self.send, self.recv = buf, send, recv
        self.copies = {}

    def go(self, number, view, peer):
        c = pltpu.make_async_remote_copy(
            src_ref=view, dst_ref=view, send_sem=self.send.at[number], recv_sem=self.recv.at[number], device_id=peer
        )
        c.start()
        self.copies[number] = c

    def got(self, *numbers):
        for n in numbers:
            self.copies[n].wait_recv()

    def step(self, s):
        buf, h, q = self.buf, N // 2, N // 4
        x, y = lax.axis_index("x"), lax.axis_index("y")
        xl, xr, yl, yr = at("x", -1), at("x", 1), at("y", -1), at("y", 1)
        top, bot = pl.ds(0, h), pl.ds(h, h)
        parts = [pl.ds(i * q, q) for i in range(4)]
        if s == 0:
            self.go(0, buf.at[x, y, top], {"x": xr})
            self.go(1, buf.at[x, y, top], {"x": xl})
            self.go(2, buf.at[x, y, bot], {"y": yr})
            self.go(3, buf.at[x, y, bot], {"y": yl})
        elif s == 1:
            self.got(0, 1, 2, 3)
            self.go(4, buf.at[xl, y, parts[0]], {"x": xr})
            self.go(5, buf.at[xr, y, parts[1]], {"x": xl})
            self.go(6, buf.at[x, yl, parts[2]], {"y": yr})
            self.go(7, buf.at[x, yr, parts[3]], {"y": yl})
        elif s == 2:
            self.got(4, 5, 6, 7)
            self.go(8, buf.at[:, y, top], {"y": yr})
            self.go(9, buf.at[:, y, top], {"y": yl})
            self.go(10, buf.at[x, :, bot], {"x": xr})
            self.go(11, buf.at[x, :, bot], {"x": xl})
        elif s == 3:
            self.got(8, 9, 10, 11)
            self.go(12, buf.at[:, yl, parts[0]], {"y": yr})
            self.go(13, buf.at[:, yr, parts[1]], {"y": yl})
            self.go(14, buf.at[xl, :, parts[2]], {"x": xr})
            self.go(15, buf.at[xr, :, parts[3]], {"x": xl})
        else:
            self.got(12, 13, 14, 15)
            for c in self.copies.values():
                c.wait_send()


class Sends:
    def __init__(self):
        self.copies = {}

    def go(self, key, src, dst, send, recv, peer):
        c = pltpu.make_async_remote_copy(
            src_ref=src, dst_ref=dst, send_sem=send, recv_sem=recv, device_id=peer
        )
        c.start()
        self.copies[key] = c

    def got(self, *keys):
        for k in keys:
            self.copies[k].wait_recv()

    def done(self):
        for c in self.copies.values():
            c.wait_send()


def column(row):
    return jnp.transpose(jnp.broadcast_to(row, (8, row.shape[1])))[:, 0:1]


def kernel(
    feats, ids, w_in_hbm, w_out_hbm, queries, qw, pos, counts,
    loss_o, gq_o, gi_o, gwi_o, gwo_o,
    w_in, w_out, q_all, u_all, nrm, ulow, unit, invlen, gs, acc, lb, plr, plc,
    snd, rcv, outb, ret, gsnd, grcv, gnb, gnret,
    gp, act_t, x_t, gh, pin, pout, ra_in, ra_out, pa_in, pa_out, rb_in, rb_out,
    st_s, st_r, bc_s, bc_r, lg,
    loc_sem, a1s, a1r, a2s, a2r, a3s, a3r, a4s, a4r, qs, qr, us, ur, sts, str_, bcs, bcr, rs_s, rs_r,
):
    x, y, z, c = (lax.axis_index(a) for a in AXES)
    barrier = pltpu.get_barrier_semaphore()
    for p in range(1, GROUP):
        pl.semaphore_signal(barrier, inc=1, device_id=z_peer(p, 1))
    for j in range(1, GROUP):
        pl.semaphore_signal(barrier, inc=1, device_id=xy_peer(j))

    load_in = pltpu.make_async_copy(w_in_hbm, w_in, loc_sem.at[0])
    load_out = pltpu.make_async_copy(w_out_hbm, w_out, loc_sem.at[1])
    load_in.start()
    load_out.start()

    f = feats[...].astype(F32)
    r = lax.rsqrt(jnp.mean(f * f, axis=1, keepdims=True) + EPS)
    nrm[...] = (f * r).astype(BF)
    idr = ids[...]
    hot = lax.broadcasted_iota(jnp.int32, (EXPERTS, N), 0) == idr
    earlier = lax.broadcasted_iota(jnp.int32, (N, N), 0) < lax.broadcasted_iota(jnp.int32, (N, N), 1)
    before = nn(hot.astype(F32).astype(BF), earlier.astype(F32).astype(BF))
    rank = jnp.sum(jnp.where(hot, before, 0.0), axis=0, keepdims=True).astype(jnp.int32)
    owner = idr >> 2
    dz = ((owner >> 1) - z) & 7
    dc = ((owner & 1) - c) & 1
    pz = jnp.where(dz <= 4, jnp.maximum(2 * dz - 1, 0), 16 - 2 * dz)
    local = idr & 3
    place = (local // EG) * GSLOTS + (pz * 2 + dc) * MSG + (local % EG) * CAP + rank
    plr[...] = place
    plc[...] = jnp.broadcast_to(column(place.astype(F32)).astype(jnp.int32), (N, D))

    def packed(values, g, i):
        slot = lax.broadcasted_iota(jnp.int32, (PACK, N), 0) + (g * GSLOTS + i * PACK)
        pick = (slot == plr[...]).astype(F32).astype(BF)
        return nn(pick, values[...]).astype(BF).reshape(PACK // MSG, EG, CAP, D)

    def unpacked(source, g):
        total = None
        for i in range(GSLOTS // D):
            slot = lax.broadcasted_iota(jnp.int32, (N, D), 1) + (g * GSLOTS + i * D)
            pick = (slot == plc[...]).astype(F32).astype(BF)
            n = D // MSG
            part = nn(pick, source[g, pl.ds(i * n, n)].reshape(D, D))
            total = part if total is None else total + part
        return total

    chunks = [(g, i) for g in range(NG) for i in reversed(range(GSLOTS // PACK))]
    n = PACK // MSG

    def pack(values, out, g, i):
        out[g, pl.ds(i * n, n)] = packed(values, g, i)

    def dispatch(sends, out, into, send, recv, g, i):
        for p in reversed(range(i * n, i * n + n)):
            if p:
                k = g * GROUP + p
                sends.go((g, p), out.at[g, p], into.at[g, p], send.at[k], recv.at[k], z_peer(p, 1))
        if i == 0:
            into[g, 0] = out[g, 0]

    def give_back(sends, out, into, send, recv, g):
        for p in reversed(range(1, GROUP)):
            k = g * GROUP + p
            sends.go((g, p), out.at[g, p], into.at[g, p], send.at[k], recv.at[k], z_peer(p, -1))
        into[g, 0] = out[g, 0]

    def group(g):
        return [(g, p) for p in range(1, GROUP)]

    gather_q = RingGather(q_all, qs, qr)
    gather_u = RingGather(u_all, us, ur)

    q_all[x, y] = queries[...]
    for g, i in chunks:
        pack(nrm, snd, g, i)
    pl.semaphore_wait(barrier, 2 * (GROUP - 1))
    sent1 = Sends()
    for g, i in chunks:
        dispatch(sent1, snd, rcv, a1s, a1r, g, i)
    gather_q.step(0)
    load_in.wait()
    load_out.wait()

    HALF = N // 2
    back2 = Sends()
    for g in range(NG):
        sent1.got(*group(g))

        def forward(k, _, g=g):
            e2, half = k // 2, lax.rem(k, 2)
            e = g * EG + e2
            rows = rcv[g, pl.ds(8 * half, 8), e2].reshape(HALF, D)
            h = nn(rows, w_in[e])
            gp[e, half] = h
            t = jnp.tanh(h * (K0 + K1 * (h * h)))
            act = (h * (0.5 + 0.5 * t)).astype(BF)
            out = nn(act, w_out[e]).astype(BF)
            outb[g, pl.ds(8 * half, 8), e2] = out.reshape(8, CAP, D)
            return _

        lax.fori_loop(0, 2 * EG, forward, 0)
        give_back(back2, outb, ret, a2s, a2r, g)
        gather_q.step(1 + g)
    for s in range(1 + NG, 4):
        gather_q.step(s)

    def keep(e, _):
        for half in range(2):
            for q in range(2):
                span = pl.ds(q * 128, 128)
                cols = pl.ds(half * HALF + q * 128, 128)
                h = gp[e, half, span]
                u = h * h
                t = jnp.tanh(h * (K0 + K1 * u))
                cdf = 0.5 + 0.5 * t
                gp[e, half, span] = cdf + (0.5 * h) * (1.0 - t * t) * (K0 + (3.0 * K1) * u)
                act_t[e, :, cols] = (h * cdf).astype(BF).T
        return _

    lax.fori_loop(0, NE, keep, 0)
    for e in range(NE):
        x_t[e] = rcv[e // EG, :, e % EG].reshape(N, D).T

    logc = jnp.log(counts[...].astype(F32))
    for d in range(GROUP):
        lg[d] = logc[:, d * N : (d + 1) * N]
    own_logc = column(lg[x * 4 + y])
    lb[...] = jnp.broadcast_to(own_logc, (N, T))

    for g in range(NG):
        back2.got(*group(g))
        if g == 0:
            acc[...] = unpacked(ret, g)
        else:
            acc[...] += unpacked(ret, g)

    summed = feats[...].astype(F32) + acc[...]
    length = jnp.sqrt(jnp.sum(summed * summed, axis=1, keepdims=True) + EPS)
    inv = 1.0 / length
    un = summed * inv
    unit[...] = un
    invlen[...] = jnp.broadcast_to(inv, (N, 128))
    ulow[...] = un.astype(BF)
    u_all[x, y] = un.astype(BF)
    gather_u.step(0)
    gather_q.step(4)

    def scores(qx, qy, t):
        return nt(ulow[...], q_all[qx, qy, pl.ds(t * T, T)]) - lb[...]

    def stat_block(j, _):
        qx, qy = lax.rem(x + j // 4, 4), lax.rem(y + lax.rem(j, 4), 4)
        for t in range(N // T):
            s = scores(qx, qy, t)
            m = jnp.max(s, axis=0, keepdims=True)
            st_s[j, 0:1, pl.ds(t * T, T)] = m
            st_s[j, 1:2, pl.ds(t * T, T)] = jnp.sum(jnp.exp(s - m), axis=0, keepdims=True)
        return _

    stats = Sends()
    for part in range(4):
        lax.fori_loop(4 * part, 4 * part + 4, stat_block, 0)
        for j in range(4 * part, 4 * part + 4):
            if j:
                stats.go(j, st_s.at[j], st_r.at[j], sts.at[j], str_.at[j], xy_peer(j))
    st_r[0] = st_s[0]
    gather_u.step(1)
    stats.got(*range(1, GROUP))
    top = jnp.max(st_r[:, 0:1, :], axis=0)
    total = jnp.sum(st_r[:, 1:2, :] * jnp.exp(st_r[:, 0:1, :] - top[None]), axis=0)
    lse = top + jnp.log(total)
    bc_s[0:1] = lse - jnp.log(qw[...])
    bc_s[1:2] = qw[...]
    bc_s[2:3] = pos[...].astype(F32)
    bc_s[3:4] = lse
    shared = Sends()
    for j in range(1, GROUP):
        shared.go(j, bc_s, bc_r.at[j], bcs.at[j], bcr.at[j], xy_peer(j))
    bc_r[0] = bc_s[...]
    gather_u.step(2)
    first_item = ((x * 4 + y) * N).astype(F32)

    acc[...] = jnp.zeros((N, D), F32)
    item_row = lax.broadcasted_iota(jnp.int32, (N, T), 0)

    def grad_block(j, _):
        qx, qy = lax.rem(x + 4 - j // 4, 4), lax.rem(y + 4 - lax.rem(j, 4), 4)
        for t in range(N // T):
            span = pl.ds(t * T, T)
            s = scores(qx, qy, t)
            e = jnp.exp(s - bc_r[j, 0:1, span])
            own = (bc_r[j, 2:3, span] - first_item).astype(jnp.int32)
            coeff = (e - jnp.where(item_row == own, bc_r[j, 1:2, span], 0.0)).astype(BF)
            acc[...] += nn(coeff, q_all[qx, qy, span])
        return _

    for part in range(4):
        shared.got(*range(max(1, 4 * part), 4 * part + 4))
        lax.fori_loop(4 * part, 4 * part + 4, grad_block, 0)
        if part == 2:
            gather_u.step(3)

    g_unit = acc[...]
    un = unit[...]
    along = jnp.sum(un * g_unit, axis=1, keepdims=True)
    gsum = (g_unit - un * along) * invlen[:, 0:1]
    gs[...] = gsum
    nrm[...] = gsum.astype(BF)
    sent3 = Sends()
    for g, i in chunks:
        pack(nrm, gsnd, g, i)
        dispatch(sent3, gsnd, grcv, a3s, a3r, g, i)

    gather_u.step(4)
    acc[...] = jnp.zeros((N, D), F32)
    lse_c = column(lse)
    weight_c = column(qw[...])
    lb[...] = jnp.broadcast_to(lse_c - jnp.log(weight_c), (N, T))
    plq = jnp.broadcast_to(column(pos[...].astype(F32)).astype(jnp.int32), (N, 128))
    weight_b = jnp.broadcast_to(weight_c, (N, 128))
    invlen[...] = jnp.zeros((N, 128), F32)

    def query_block(d, _):
        ix, iy = d // 4, lax.rem(d, 4)
        for t in range(N // 128):
            span = pl.ds(t * 128, 128)
            s = nt(queries[...], u_all[ix, iy, span]) - lg[d, :, span]
            e = jnp.exp(s - lb[:, 0:128])
            hit = lax.broadcasted_iota(jnp.int32, (N, 128), 1) + (d * N + t * 128) == plq
            coeff = (e - jnp.where(hit, weight_b, 0.0)).astype(BF)
            invlen[...] += jnp.where(hit, s, 0.0)
            acc[...] += nn(coeff, u_all[ix, iy, span])
        return _

    lax.fori_loop(0, QCUT, query_block, 0)

    back4 = Sends()
    rs = Sends()

    def reduce_go(g, number, src, dst, peer):
        rs.go((g, number), src, dst, rs_s.at[g * 12 + number], rs_r.at[g * 12 + number], peer)

    for g in range(NG):
        sent3.got(*group(g))

        def backward(k, _, g=g):
            e2, half = k // 2, lax.rem(k, 2)
            e = g * EG + e2
            rows = grcv[g, pl.ds(8 * half, 8), e2].reshape(HALF, D)
            ghv = (nt(rows, w_out[e]) * gp[e, half]).astype(BF)
            gh[e, half] = ghv
            gnb[g, pl.ds(8 * half, 8), e2] = nt(ghv, w_in[e]).astype(BF).reshape(8, CAP, D)
            return _

        lax.fori_loop(0, 2 * EG, backward, 0)
        give_back(back4, gnb, gnret, a4s, a4r, g)

        def weights(e2, _, g=g):
            e = g * EG + e2
            pin[g, :, :, e2] = nn(x_t[e], gh[e].reshape(N, FF)).astype(BF).reshape(4, 4, 16, FF)
            rows = grcv[g, :, e2].reshape(N, D)
            pout[g, :, :, e2] = nn(act_t[e], rows).astype(BF).reshape(4, 4, 64, D)
            return _

        lax.fori_loop(0, EG, weights, 0)
        for k in (1, 3, 2):
            reduce_go(g, k - 1, pin.at[g, at("x", k)], ra_in.at[g, k - 1], {"x": at("x", k)})
            reduce_go(g, k + 2, pout.at[g, :, at("y", k)], ra_out.at[g, k - 1], {"y": at("y", k)})
    lax.fori_loop(QCUT, GROUP, query_block, 0)
    gq_o[...] = acc[...]
    picked = jnp.sum(invlen[...], axis=1, keepdims=True)
    loss_o[...] = jnp.transpose(jnp.broadcast_to(lse_c - picked, (N, 128)))[0:1]

    def first_sums(g):
        rs.got(*[(g, n) for n in range(6)])
        for k in range(4):
            t = pin[g, x, k].astype(F32)
            u = pout[g, k, y].astype(F32)
            for i in range(3):
                t = t + ra_in[g, i, k].astype(F32)
                u = u + ra_out[g, i, k].astype(F32)
            pa_in[g, k] = t.astype(BF)
            pa_out[g, k] = u.astype(BF)
        for k in (1, 3, 2):
            reduce_go(g, k + 5, pa_in.at[g, at("y", k)], rb_in.at[g, k - 1], {"y": at("y", k)})
            reduce_go(g, k + 8, pa_out.at[g, at("x", k)], rb_out.at[g, k - 1], {"x": at("x", k)})

    def last_sums(g):
        rs.got(*[(g, n) for n in range(6, 12)])
        t = pa_in[g, y].astype(F32)
        u = pa_out[g, x].astype(F32)
        for i in range(3):
            t = t + rb_in[g, i].astype(F32)
            u = u + rb_out[g, i].astype(F32)
        gwi_o[pl.ds(g * EG, EG)] = t
        gwo_o[pl.ds(g * EG, EG)] = u

    for g in range(NG):
        first_sums(g)
    for g in range(NG):
        back4.got(*group(g))
        if g == 0:
            acc[...] = unpacked(gnret, g)
        else:
            acc[...] += unpacked(gnret, g)
        if g < NG - 1:
            last_sums(g)
    f = feats[...].astype(F32)
    r = lax.rsqrt(jnp.mean(f * f, axis=1, keepdims=True) + EPS)
    grows = acc[...]
    projected = jnp.mean(grows * f, axis=1, keepdims=True)
    gi_o[...] = gs[...] + r * (grows - f * (r * r * projected))
    last_sums(NG - 1)
    for sends in (sent1, back2, stats, shared, sent3, back4, rs):
        sends.done()


def finishing(loss, gq, gi, gwi, gwo, loss_o, gq_o, gi_o, gwi_o, gwo_o):
    loss_o[...] = loss[...]
    gq_o[...] = gq[...]
    gi_o[...] = gi[...]
    for e in range(NE):
        gwi_o[:, e, :] = gwi[e]
        gwo_o[:, e, :] = gwo[e]


def per_device(feats, ids, w_in, w_out, queries, qw, pos, counts):
    vm = pl.BlockSpec(memory_space=pltpu.VMEM)
    hbm = pl.BlockSpec(memory_space=pl.ANY)
    V = pltpu.VMEM
    sem = pltpu.SemaphoreType.DMA
    slots = (NG, GROUP, EG, CAP, D)
    many = sem((NG * GROUP,))
    scratch = [
        V((NE, D, FF), BF), V((NE, FF, D), BF), V((4, 4, N, D), BF), V((4, 4, N, D), BF),
        V((N, D), BF), V((N, D), BF), V((N, D), F32), V((N, 128), F32), V((N, D), F32), V((N, D), F32), V((N, T), F32),
        V((1, N), jnp.int32), V((N, D), jnp.int32),
        *[V(slots, BF) for _ in range(8)],
        V((NE, 2, N // 2, FF), F32), V((NE, FF, N), BF), V((NE, D, N), BF), V((NE, 2, N // 2, FF), BF),
        V((NG, 4, 4, EG, 16, FF), BF), V((NG, 4, 4, EG, 64, D), BF),
        V((NG, 3, 4, EG, 16, FF), BF), V((NG, 3, 4, EG, 64, D), BF),
        V((NG, 4, EG, 16, FF), BF), V((NG, 4, EG, 64, D), BF),
        V((NG, 3, EG, 16, FF), BF), V((NG, 3, EG, 64, D), BF),
        V((GROUP, 2, N), F32), V((GROUP, 2, N), F32), V((4, N), F32), V((GROUP, 4, N), F32), V((GROUP, 1, N), F32),
        sem((2,)), *[many for _ in range(8)], *[sem((GROUP,)) for _ in range(8)], sem((NG * 12,)), sem((NG * 12,)),
    ]
    made = (
        jax.ShapeDtypeStruct((1, N), F32),
        jax.ShapeDtypeStruct((N, D), F32),
        jax.ShapeDtypeStruct((N, D), F32),
        jax.ShapeDtypeStruct((NE, 16, FF), F32),
        jax.ShapeDtypeStruct((NE, 64, D), F32),
    )
    results = pl.pallas_call(
        kernel,
        out_shape=made,
        in_specs=[vm, vm, hbm, hbm, vm, vm, vm, vm],
        out_specs=[vm] * 5,
        scratch_shapes=scratch,
        compiler_params=pltpu.CompilerParams(
            collective_id=0, has_side_effects=True, vmem_limit_bytes=60 << 20
        ),
        name="tower_step",
    )(feats[0], ids.reshape(1, N), w_in, w_out, queries[0], qw, pos, counts)
    outs = (*made[:3], jax.ShapeDtypeStruct((16, NE, FF), F32), jax.ShapeDtypeStruct((64, NE, D), F32))
    loss, gq, gi, gwi, gwo = pl.pallas_call(
        finishing, out_shape=outs, in_specs=[vm] * 5, out_specs=[vm] * 5, name="write_out"
    )(*results)
    return (loss, gq[None], gi[None], gwi, gwo)


def solution(mesh):
    torus = Mesh(mesh.devices.reshape(4, 4, 8, 2), AXES)
    dp, ex = ("x", "y"), ("z", "c")
    in_specs = (
        P(ex, dp, None), P(ex, dp, None), P(ex, None, None), P(ex, None, None),
        P(ex, dp, None), P(ex, dp), P(ex, dp), P(ex, None),
    )
    out_specs = (
        P(ex, dp), P(ex, dp, None), P(ex, dp, None), P(dp, ex, None), P(dp, ex, None),
    )
    return jax.shard_map(
        per_device, mesh=torus, in_specs=in_specs, out_specs=out_specs, check_vma=False
    )
```

time: 188 us -> 149 us (0.79)
  Pallas kernels: 173 us -> 146 us
  local copies, waits for them, and re-layouts: 13.1 us -> 0 us
    pallas_call x1 -> x2, Pallas kernels: 173 us -> 146 us  [the longest x1 144 us: per_device(): pl.pallas_call(kernel, out_shape=made, in_specs=[vm, vm, hbm, hbm, vm, vm...]
    unnamed x9 -> x0, local copies, waits for them, and re-layouts: 7.63 us -> none
    reshape x4 -> x0, local copies, waits for them, and re-layouts: 3.94 us -> none  [the longest x1 1.53 us: per_device(): pos.reshape(N, 1)]
where the time goes in v2:
time: 149 us; the launch traced here: 147 us
  Pallas kernels  146 us (98%)
    pallas_call x1, Pallas kernels, per_device(): pl.pallas_call(kernel, out_shape=made, in_specs=[vm, vm, hbm, hbm, vm, vm...  144 us

profile of v2, /device:TPU:24, one launch (start us, length us, event | category | flops | bytes accessed | tf_op | source)
XLA Modules:
  0.0 147.1 jit_solution(9665402695708615330)
XLA Ops:
  0.6 143.9 %tower_step.1 = (f32[1,512]{1,0:T(1,128)}, f32[512,256]{1,0:T(8,128)}, f32[512,256]{1,0:T(8,128)}, f32[4,16,1024]{2,1,0:T(8,128)}, f32[4,64,256]{2,1,0:T(8,128)}) custom-call(bf16[512,256]{1,0:T(8,128)(2,1)} %bitcast.5, s32[1,512]{1,0:T(1,128)} %bitcast.7, bf16[4,256,1024]{2,1,0:T(8,128)(2,1)} %w_in_hbm.1, bf16[4,1024,256]{2,1,0:T(8,128)(2,1)} %w_out_hbm.1, ...), custom_call_target="tpu_custom_call" | custom-call | tf_op jit(solution)/shard_map/tower_step/pallas_call | solution.py:493
  144.6 2.5 %write_out.1 = (f32[1,512]{1,0:T(1,128)}, f32[512,256]{1,0:T(8,128)}, f32[512,256]{1,0:T(8,128)}, f32[16,4,1024]{2,1,0:T(4,128)}, f32[64,4,256]{2,1,0:T(4,128)}) custom-call(f32[1,512]{1,0:T(1,128)} %get-tuple-element.15.loss, f32[512,256]{1,0:T(8,128)} %get-tuple-element.16.gq, f32[512,256]{1,0:T(8,128)} %get-tuple-element.17.gi, ...), custom_call_target="tpu_custom_call" | custom-call | tf_op jit(solution)/shard_map/write_out/pallas_call | solution.py:505

commit v3 on v2

--- a/solution.py
+++ b/solution.py
@@ -240,9 +240,6 @@
         lax.fori_loop(0, 2 * EG, forward, 0)
         give_back(back2, outb, ret, a2s, a2r, g)
         gather_q.step(1 + g)
-    for s in range(1 + NG, 4):
-        gather_q.step(s)
-
     def keep(e, _):
         for half in range(2):
             for q in range(2):
@@ -257,6 +254,7 @@
         return _
 
     lax.fori_loop(0, NE, keep, 0)
+    gather_q.step(3)
     for e in range(NE):
         x_t[e] = rcv[e // EG, :, e % EG].reshape(N, D).T
 
@@ -298,7 +296,7 @@
 
     stats = Sends()
     for part in range(4):
-        lax.fori_loop(4 * part, 4 * part + 4, stat_block, 0)
+        lax.fori_loop(4 * part, 4 * part + 4, stat_block, 0, unroll=True)
         for j in range(4 * part, 4 * part + 4):
             if j:
                 stats.go(j, st_s.at[j], st_r.at[j], sts.at[j], str_.at[j], xy_peer(j))
@@ -335,9 +333,7 @@
 
     for part in range(4):
         shared.got(*range(max(1, 4 * part), 4 * part + 4))
-        lax.fori_loop(4 * part, 4 * part + 4, grad_block, 0)
-        if part == 2:
-            gather_u.step(3)
+        lax.fori_loop(4 * part, 4 * part + 4, grad_block, 0, unroll=True)
 
     g_unit = acc[...]
     un = unit[...]
@@ -350,7 +346,8 @@
         pack(nrm, gsnd, g, i)
         dispatch(sent3, gsnd, grcv, a3s, a3r, g, i)
 
-    gather_u.step(4)
+    gather_u.step(3)
+
     acc[...] = jnp.zeros((N, D), F32)
     lse_c = column(lse)
     weight_c = column(qw[...])
@@ -371,8 +368,6 @@
             acc[...] += nn(coeff, u_all[ix, iy, span])
         return _
 
-    lax.fori_loop(0, QCUT, query_block, 0)
-
     back4 = Sends()
     rs = Sends()
 
@@ -405,7 +400,9 @@
         for k in (1, 3, 2):
             reduce_go(g, k - 1, pin.at[g, at("x", k)], ra_in.at[g, k - 1], {"x": at("x", k)})
             reduce_go(g, k + 2, pout.at[g, :, at("y", k)], ra_out.at[g, k - 1], {"y": at("y", k)})
-    lax.fori_loop(QCUT, GROUP, query_block, 0)
+        if g == 0:
+            gather_u.step(4)
+        lax.fori_loop(g * QCUT, (g + 1) * QCUT, query_block, 0)
     gq_o[...] = acc[...]
     picked = jnp.sum(invlen[...], axis=1, keepdims=True)
     loss_o[...] = jnp.transpose(jnp.broadcast_to(lse_c - picked, (N, 128)))[0:1]

time: 149 us -> 138 us (0.926); the launches traced: 147 us -> 138 us
  Pallas kernels: 146 us -> 137 us
    pallas_call x1, Pallas kernels: 144 us -> 135 us  [per_device(): pl.pallas_call(kernel, out_shape=made, in_specs=[vm, vm, hbm, hbm, vm, vm...]
where the time goes in v3:
time: 138 us
  Pallas kernels  137 us (99%)
    pallas_call x1, Pallas kernels, per_device(): pl.pallas_call(kernel, out_shape=made, in_specs=[vm, vm, hbm, hbm, vm, vm...  135 us

profile of v3, /device:TPU:24, one launch (start us, length us, event | category | flops | bytes accessed | tf_op | source)
XLA Modules:
  0.0 137.7 jit_solution(11256377167643828430)
XLA Ops:
  0.6 134.5 %tower_step.1 = (f32[1,512]{1,0:T(1,128)}, f32[512,256]{1,0:T(8,128)}, f32[512,256]{1,0:T(8,128)}, f32[4,16,1024]{2,1,0:T(8,128)}, f32[4,64,256]{2,1,0:T(8,128)}) custom-call(bf16[512,256]{1,0:T(8,128)(2,1)} %bitcast.5, s32[1,512]{1,0:T(1,128)} %bitcast.7, bf16[4,256,1024]{2,1,0:T(8,128)(2,1)} %w_in_hbm.1, bf16[4,1024,256]{2,1,0:T(8,128)(2,1)} %w_out_hbm.1, ...), custom_call_target="tpu_custom_call" | custom-call | tf_op jit(solution)/shard_map/tower_step/pallas_call | solution.py:490
  135.2 2.5 %write_out.1 = (f32[1,512]{1,0:T(1,128)}, f32[512,256]{1,0:T(8,128)}, f32[512,256]{1,0:T(8,128)}, f32[16,4,1024]{2,1,0:T(4,128)}, f32[64,4,256]{2,1,0:T(4,128)}) custom-call(f32[1,512]{1,0:T(1,128)} %get-tuple-element.15.loss, f32[512,256]{1,0:T(8,128)} %get-tuple-element.16.gq, f32[512,256]{1,0:T(8,128)} %get-tuple-element.17.gi, ...), custom_call_target="tpu_custom_call" | custom-call | tf_op jit(solution)/shard_map/write_out/pallas_call | solution.py:502

commit v4 on v3

--- a/solution.py
+++ b/solution.py
@@ -24,7 +24,7 @@
 MSG = EG * CAP
 GSLOTS = GROUP * MSG
 T = 256
-QCUT = 8
+QCUT = (0, 4, 16)
 PACK = 512
 EPS = 1e-6
 K0 = math.sqrt(2.0 / math.pi)
@@ -331,9 +331,9 @@
             acc[...] += nn(coeff, q_all[qx, qy, span])
         return _
 
-    for part in range(4):
-        shared.got(*range(max(1, 4 * part), 4 * part + 4))
-        lax.fori_loop(4 * part, 4 * part + 4, grad_block, 0, unroll=True)
+    for first, last in ((0, 1), (1, 4), (4, 8), (8, 12), (12, 16)):
+        shared.got(*range(max(1, first), last))
+        lax.fori_loop(first, last, grad_block, 0, unroll=True)
 
     g_unit = acc[...]
     un = unit[...]
@@ -402,7 +402,7 @@
             reduce_go(g, k + 2, pout.at[g, :, at("y", k)], ra_out.at[g, k - 1], {"y": at("y", k)})
         if g == 0:
             gather_u.step(4)
-        lax.fori_loop(g * QCUT, (g + 1) * QCUT, query_block, 0)
+        lax.fori_loop(QCUT[g], QCUT[g + 1], query_block, 0)
     gq_o[...] = acc[...]
     picked = jnp.sum(invlen[...], axis=1, keepdims=True)
     loss_o[...] = jnp.transpose(jnp.broadcast_to(lse_c - picked, (N, 128)))[0:1]

time: 138 us -> 138 us (level)
  no operation moved by 1% of the time
where the time goes in v4:
time: 138 us; the launch traced here: 136 us
  Pallas kernels  136 us (99%)
    pallas_call x1, Pallas kernels, per_device(): pl.pallas_call(kernel, out_shape=made, in_specs=[vm, vm, hbm, hbm, vm, vm...  133 us

profile of v4, /device:TPU:24, one launch (start us, length us, event | category | flops | bytes accessed | tf_op | source)
XLA Modules:
  0.0 136.3 jit_solution(9249143073670767871)
XLA Ops:
  0.6 133.2 %tower_step.1 = (f32[1,512]{1,0:T(1,128)}, f32[512,256]{1,0:T(8,128)}, f32[512,256]{1,0:T(8,128)}, f32[4,16,1024]{2,1,0:T(8,128)}, f32[4,64,256]{2,1,0:T(8,128)}) custom-call(bf16[512,256]{1,0:T(8,128)(2,1)} %bitcast.5, s32[1,512]{1,0:T(1,128)} %bitcast.7, bf16[4,256,1024]{2,1,0:T(8,128)(2,1)} %w_in_hbm.1, bf16[4,1024,256]{2,1,0:T(8,128)(2,1)} %w_out_hbm.1, ...), custom_call_target="tpu_custom_call" | custom-call | tf_op jit(solution)/shard_map/tower_step/pallas_call | solution.py:490
  133.8 2.5 %write_out.1 = (f32[1,512]{1,0:T(1,128)}, f32[512,256]{1,0:T(8,128)}, f32[512,256]{1,0:T(8,128)}, f32[16,4,1024]{2,1,0:T(4,128)}, f32[64,4,256]{2,1,0:T(4,128)}) custom-call(f32[1,512]{1,0:T(1,128)} %get-tuple-element.15.loss, f32[512,256]{1,0:T(8,128)} %get-tuple-element.16.gq, f32[512,256]{1,0:T(8,128)} %get-tuple-element.17.gi, ...), custom_call_target="tpu_custom_call" | custom-call | tf_op jit(solution)/shard_map/write_out/pallas_call | solution.py:502
